TPU v7x, 32 devices: a whole 2x2x4 slice. The times are simulated.
32 devices in a mesh: shard: 4 (over y, x), ctx: 4 (over z), tp: 2 (over core).
Axes of the slice: x: 2, y: 2, z: 4, core: 2. Of those that a mesh axis runs over, the one named last changes fastest.
Arguments:
- inputs: bfloat16 [4, 512, 1024], P('shard', 'ctx'), may hold values from -6 to 6
- cotangent: bfloat16 [4, 512, 1024], P('shard', 'ctx'), may hold values from -6 to 6
- mixer_matrix: float32 [1024, 4, 1024], P(('shard', 'ctx', 'tp')), may hold values from -0.1875 to 0.1875
- ffn_weight: float32 [4608, 3, 1024], P(('shard', 'ctx', 'tp')), may hold values from -0.1875 to 0.1875
- conv_weight: float32 [3, 1024], replicated, may hold values from -3.5 to 3.5
- norm_gains: float32 [2, 1024], replicated, may hold values from 0.5 to 1.5
- mixer_first: float32 [1024, 4, 1024], P(('shard', 'ctx', 'tp')), as said below
- mixer_second: float32 [1024, 4, 1024], P(('shard', 'ctx', 'tp')), as said below
- ffn_first: float32 [4608, 3, 1024], P(('shard', 'ctx', 'tp')), as said below
- ffn_second: float32 [4608, 3, 1024], P(('shard', 'ctx', 'tp')), as said below
- conv_first: float32 [3, 1024], replicated, as said below
- conv_second: float32 [3, 1024], replicated, as said below
- gain_first: float32 [2, 1024], replicated, as said below
- gain_second: float32 [2, 1024], replicated, as said below
Outputs:
- output: bfloat16 [4, 512, 1024], P('shard', 'ctx')
- input_grad: float32 [4, 512, 1024], P('shard', 'ctx')
- mixer_grad: float32 [1024, 4, 1024], P(('shard', 'ctx', 'tp'))
- ffn_grad: float32 [4608, 3, 1024], P(('shard', 'ctx', 'tp'))
- conv_grad: float32 [3, 1024], replicated
- gain_grad: float32 [2, 1024], replicated
- mixer_new: float32 [1024, 4, 1024], P(('shard', 'ctx', 'tp'))
- ffn_new: float32 [4608, 3, 1024], P(('shard', 'ctx', 'tp'))
- conv_new: float32 [3, 1024], replicated
- gain_new: float32 [2, 1024], replicated
- mixer_first_new: float32 [1024, 4, 1024], P(('shard', 'ctx', 'tp'))
- mixer_second_new: float32 [1024, 4, 1024], P(('shard', 'ctx', 'tp'))
- ffn_first_new: float32 [4608, 3, 1024], P(('shard', 'ctx', 'tp'))
- ffn_second_new: float32 [4608, 3, 1024], P(('shard', 'ctx', 'tp'))
- conv_first_new: float32 [3, 1024], replicated
- conv_second_new: float32 [3, 1024], replicated
- gain_first_new: float32 [2, 1024], replicated
- gain_second_new: float32 [2, 1024], replicated
Inputs may be any that keep to these rules, and one draw needn't show every extreme that they name: `mixer_first`: a running mean of earlier gradients. `mixer_second`: a running mean of squared earlier gradients. `ffn_first`: a running mean of earlier gradients. `ffn_second`: a running mean of squared earlier gradients. `conv_first`: a running mean of earlier gradients. `conv_second`: a running mean of squared earlier gradients. `gain_first`: a running mean of earlier gradients. `gain_second`: a running mean of squared earlier gradients.
All inputs are finite; a program needn't handle non-finite values.
Results may differ from a plain program's by a relative error of at most 0.009.
The roundings to bfloat16 on the way count: a program that leaves them out, or rounds other values in their place, can miss the bound.
Values may be sent and summed in bfloat16 or wider, within the bound.
No kernel may reach another device: no remote copies, remote signals or barrier semaphores. Data moves between devices by JAX's collectives and lax.ppermute only.
A program may use at most 192 MiB of HBM per device.

v0:
```python
import jax
import jax.numpy as jnp
from jax import lax
from jax.sharding import PartitionSpec as P

STEP = 10
norm_eps = 1e-05
beta_first = 0.9
beta_second = 0.999
adam_eps = 1e-08
matrix_rate = 0.02
small_rate = 0.25
decay_rate = 0.1


def shifted(value, axis, steps):
    count = lax.axis_size(axis)
    leading, last = (max(0, -steps), min(count, count - steps))
    return lax.ppermute(value, axis, [(source, source + steps) for source in range(leading, last)])


def rms_scale(values):
    return lax.rsqrt(jnp.mean(values * values, axis=-1, keepdims=True) + norm_eps)


def norm_backward(grad_normed, normed, scale):
    return scale * (grad_normed - normed * jnp.mean(grad_normed * normed, axis=-1, keepdims=True))


def adam_update(weight, gradient, first, second, rate, decay):
    first_new = beta_first * first + (1.0 - beta_first) * gradient
    second_new = beta_second * second + (1.0 - beta_second) * gradient * gradient
    first_hat = first_new / (1.0 - beta_first**STEP)
    second_hat = second_new / (1.0 - beta_second**STEP)
    weight_new = weight - rate * (first_hat / (jnp.sqrt(second_hat) + adam_eps) + decay * weight)
    return (weight_new, first_new, second_new)


def group_layout(model_width):
    tp_count = lax.axis_size("tp")
    group_count = lax.axis_size("shard") * lax.axis_size("ctx")
    return (tp_count, group_count, model_width // (group_count * tp_count))


def own_taps(conv_weight):
    tp_count, group_count, block_size = group_layout(conv_weight.shape[1])
    grouped = conv_weight.reshape(3, group_count, tp_count, block_size)
    picked = lax.dynamic_index_in_dim(grouped, lax.axis_index("tp"), axis=2, keepdims=False)
    return picked.reshape(3, group_count * block_size)


def spread_taps(tap_grads, model_width):
    tp_count, group_count, block_size = group_layout(model_width)
    blank_grid = jnp.zeros((3, group_count, tp_count, block_size), jnp.float32)
    placed = lax.dynamic_update_index_in_dim(
        blank_grid, tap_grads.reshape(3, group_count, block_size), lax.axis_index("tp"), 2
    )
    return placed.reshape(3, model_width)


def reduce_terms(inner_term, outer_term):
    moved_in, moved_out = (
        lax.all_to_all(
            inner_term[None].astype(jnp.bfloat16),
            ("shard", "ctx"),
            split_axis=1,
            concat_axis=0,
            tiled=True,
        ).astype(jnp.float32),
        lax.all_to_all(
            outer_term[None].astype(jnp.bfloat16),
            ("shard", "ctx"),
            split_axis=1,
            concat_axis=0,
            tiled=True,
        ).astype(jnp.float32),
    )
    summed_in = jnp.sum(moved_in, axis=0)
    summed_out = jnp.sum(moved_out, axis=0)
    return jnp.concatenate([summed_in, summed_out[:, None, :]], axis=1)


def per_device(
    inputs,
    cotangent,
    mixer_matrix,
    ffn_weight,
    conv_weight,
    norm_gains,
    mixer_first,
    mixer_second,
    ffn_first,
    ffn_second,
    conv_first,
    conv_second,
    gain_first,
    gain_second,
):
    seq_count, tok_count, model_width = inputs.shape
    row_count = seq_count * tok_count
    mixer_half = mixer_matrix.astype(jnp.bfloat16)
    ffn_half = ffn_weight.astype(jnp.bfloat16)
    mixer_whole, ffn_whole = (
        lax.all_gather(mixer_half, ("shard", "ctx"), axis=0, tiled=True),
        lax.all_gather(ffn_half, ("shard", "ctx"), axis=0, tiled=True),
    )
    channel_count = mixer_whole.shape[0]
    x_rows = inputs.reshape(row_count, model_width).astype(jnp.float32)
    scale_one = rms_scale(x_rows)
    normed_one = x_rows * scale_one
    h_one = (normed_one * norm_gains[0]).astype(jnp.bfloat16)
    h_seqs = h_one.reshape(seq_count, tok_count, model_width)
    before = shifted(h_seqs[:, tok_count - 2 :, :], "ctx", 1)
    fwd_rows = jnp.concatenate([before, h_seqs], axis=1).reshape(
        seq_count * (tok_count + 2), model_width
    )
    taps_own = own_taps(conv_weight)
    projected = jnp.einsum(
        "rd,ckd->rkc", fwd_rows, mixer_whole[:, :3, :], preferred_element_type=jnp.float32
    )
    projected = projected.reshape(seq_count, tok_count + 2, 3, channel_count)
    in_b = projected[:, :, 0, :]
    in_x = projected[:, :, 2, :]
    in_c = projected[:, 2:, 1, :]
    product = in_b * in_x
    mixed_rows = (
        taps_own[0] * product[:, :tok_count]
        + taps_own[1] * product[:, 1 : tok_count + 1]
        + taps_own[2] * product[:, 2:]
    )
    gated_row_block = (in_c * mixed_rows).astype(jnp.bfloat16).reshape(row_count, channel_count)
    mix_part = jnp.dot(gated_row_block, mixer_whole[:, 3, :], preferred_element_type=jnp.float32)
    mix_out = lax.psum(mix_part, "tp")
    residual = x_rows + mix_out
    scale_two = rms_scale(residual)
    normed_two = residual * scale_two
    h_two = (normed_two * norm_gains[1]).astype(jnp.bfloat16)
    gate_and_lift = jnp.einsum(
        "rd,ckd->rkc", h_two, ffn_whole[:, :2, :], preferred_element_type=jnp.float32
    )
    gate_pre = gate_and_lift[:, 0, :]
    up_value = gate_and_lift[:, 1, :]
    sigmoid_gate = jax.nn.sigmoid(gate_pre)
    gate_act = gate_pre * sigmoid_gate
    hidden = (gate_act * up_value).astype(jnp.bfloat16)
    ffn_part = jnp.dot(hidden, ffn_whole[:, 2, :], preferred_element_type=jnp.float32)
    ffn_out = lax.psum(ffn_part.astype(jnp.bfloat16), "tp").astype(jnp.float32)
    output = (residual + ffn_out).astype(jnp.bfloat16).reshape(inputs.shape)
    mixer_backward, ffn_back = (
        lax.all_gather(mixer_half, ("shard", "ctx"), axis=0, tiled=True),
        lax.all_gather(ffn_half, ("shard", "ctx"), axis=0, tiled=True),
    )
    grad_rows = cotangent.reshape(row_count, model_width)
    grad_float = grad_rows.astype(jnp.float32)
    grad_hidden = jnp.einsum(
        "rd,cd->rc", grad_rows, ffn_back[:, 2, :], preferred_element_type=jnp.float32
    )
    grad_gate = (
        grad_hidden * up_value * sigmoid_gate * (1.0 + gate_pre * (1.0 - sigmoid_gate))
    ).astype(jnp.bfloat16)
    grad_up = (grad_hidden * gate_act).astype(jnp.bfloat16)
    grad_pair = jnp.stack([grad_gate, grad_up], axis=1)
    part_two = jnp.einsum(
        "rkc,ckd->rd", grad_pair, ffn_back[:, :2, :], preferred_element_type=jnp.float32
    )
    grad_h_two = lax.psum(part_two, "tp")
    ffn_inner = jnp.einsum("rkc,rd->ckd", grad_pair, h_two, preferred_element_type=jnp.float32)
    ffn_outer = jnp.einsum("rc,rd->cd", hidden, grad_rows, preferred_element_type=jnp.float32)
    ffn_grad = reduce_terms(ffn_inner, ffn_outer)
    grad_resid = grad_float + norm_backward(grad_h_two * norm_gains[1], normed_two, scale_two)
    grad_mix = grad_resid.astype(jnp.bfloat16)
    grad_seqs = grad_mix.reshape(seq_count, tok_count, model_width)
    following_hidden, next_grad = shifted((h_seqs[:, :2, :], grad_seqs[:, :2, :]), "ctx", -1)
    grad_ext = jnp.concatenate([grad_seqs, next_grad], axis=1).reshape(
        seq_count * (tok_count + 2), model_width
    )
    c_next = jnp.einsum(
        "qxe,ae->qxa", following_hidden, mixer_backward[:, 1, :], preferred_element_type=jnp.float32
    )
    c_ext = jnp.concatenate([in_c, c_next], axis=1)
    grad_gated = jnp.einsum(
        "rd,cd->rc", grad_ext, mixer_backward[:, 3, :], preferred_element_type=jnp.float32
    )
    grad_gated = grad_gated.reshape(seq_count, tok_count + 2, channel_count)
    grad_mixed = grad_gated * c_ext
    grad_c = grad_gated[:, :tok_count] * mixed_rows
    grad_prod = (
        taps_own[2] * grad_mixed[:, :tok_count]
        + taps_own[1] * grad_mixed[:, 1 : tok_count + 1]
        + taps_own[0] * grad_mixed[:, 2:]
    )
    grad_b = grad_prod * in_x[:, 2:]
    grad_x = grad_prod * in_b[:, 2:]
    gradient_triple = (
        jnp.stack([grad_b, grad_c, grad_x], axis=2)
        .astype(jnp.bfloat16)
        .reshape(row_count, 3, channel_count)
    )
    part_one = jnp.einsum(
        "rkc,ckd->rd", gradient_triple, mixer_backward[:, :3, :], preferred_element_type=jnp.float32
    )
    own_mixed = grad_mixed[:, :tok_count]
    tap_zero = jnp.sum(own_mixed * product[:, :tok_count], axis=(0, 1))
    tap_one = jnp.sum(own_mixed * product[:, 1 : tok_count + 1], axis=(0, 1))
    tap_two = jnp.sum(own_mixed * product[:, 2:], axis=(0, 1))
    tap_grads = jnp.stack([tap_zero, tap_one, tap_two])
    grad_h_one = lax.psum(part_one.astype(jnp.bfloat16), "tp").astype(jnp.float32)
    mixer_inner = jnp.einsum(
        "rkc,rd->ckd", gradient_triple, h_one, preferred_element_type=jnp.float32
    )
    mixer_outer = jnp.einsum(
        "rc,rd->cd", gated_row_block, grad_mix, preferred_element_type=jnp.float32
    )
    mixer_grad = reduce_terms(mixer_inner, mixer_outer)
    gain_terms = jnp.stack(
        [jnp.sum(part_one * normed_one, axis=0), jnp.sum(part_two * normed_two, axis=0)]
    )
    gain_grad, conv_grad = lax.psum(
        (gain_terms, spread_taps(tap_grads, model_width)), ("shard", "ctx", "tp")
    )
    input_grad = grad_resid + norm_backward(grad_h_one * norm_gains[0], normed_one, scale_one)
    input_grad = input_grad.reshape(inputs.shape)
    mixer_new, mixer_first_new, mixer_second_new = adam_update(
        mixer_matrix, mixer_grad, mixer_first, mixer_second, matrix_rate, decay_rate
    )
    ffn_new, ffn_first_new, ffn_second_new = adam_update(
        ffn_weight, ffn_grad, ffn_first, ffn_second, matrix_rate, decay_rate
    )
    conv_new, conv_first_new, conv_second_new = adam_update(
        conv_weight, conv_grad, conv_first, conv_second, small_rate, 0.0
    )
    gain_new, gain_first_new, gain_second_new = adam_update(
        norm_gains, gain_grad, gain_first, gain_second, small_rate, 0.0
    )
    return (
        output,
        input_grad,
        mixer_grad,
        ffn_grad,
        conv_grad,
        gain_grad,
        mixer_new,
        ffn_new,
        conv_new,
        gain_new,
        mixer_first_new,
        mixer_second_new,
        ffn_first_new,
        ffn_second_new,
        conv_first_new,
        conv_second_new,
        gain_first_new,
        gain_second_new,
    )


def solution(mesh):
    in_specs = (
        P("shard", "ctx", None),
        P("shard", "ctx", None),
        P(("shard", "ctx", "tp"), None, None),
        P(("shard", "ctx", "tp"), None, None),
        P(),
        P(),
        P(("shard", "ctx", "tp"), None, None),
        P(("shard", "ctx", "tp"), None, None),
        P(("shard", "ctx", "tp"), None, None),
        P(("shard", "ctx", "tp"), None, None),
        P(),
        P(),
        P(),
        P(),
    )
    out_specs = (
        P("shard", "ctx", None),
        P("shard", "ctx", None),
        P(("shard", "ctx", "tp"), None, None),
        P(("shard", "ctx", "tp"), None, None),
        P(),
        P(),
        P(("shard", "ctx", "tp"), None, None),
        P(("shard", "ctx", "tp"), None, None),
        P(),
        P(),
        P(("shard", "ctx", "tp"), None, None),
        P(("shard", "ctx", "tp"), None, None),
        P(("shard", "ctx", "tp"), None, None),
        P(("shard", "ctx", "tp"), None, None),
        P(),
        P(),
        P(),
        P(),
    )
    return jax.shard_map(
        per_device, mesh=mesh, in_specs=in_specs, out_specs=out_specs, check_vma=False
    )
```

profile of v0, /device:TPU:0, one launch (start us, length us, event | category | flops | bytes accessed | tf_op | source)
XLA Modules:
  0.0 928.6 jit_solution(14838838235188853788)
XLA Ops:
  12.9 5.0 collective-permute-start
  19.2 70.4 %all-gather.3.cloned.1.call-done = bf16[512,4,1024]{2,0,1:T(8,128)(2,1)} async-done(((bf16[32,4,1024]{2,0,1:T(8,128)(2,1)}), bf16[512,4,1024]{2,0,1:T(8,128)(2,1)}) %all-gather.3.cloned.1.call-update) | async-done | bytes 4194320 | tf_op jit(solution)/shard_map/all_gather | solution.py:104
  97.9 16.2 %all-reduce.6.cloned.1.call-done = f32[128,1024]{1,0:T(8,128)} async-done(((f32[128,1024]{1,0:T(8,128)}), f32[128,1024]{1,0:T(8,128)}) %all-reduce.6.cloned.1.call-update) | async-done | bytes 524304 | tf_op jit(solution)/shard_map/psum | solution.py:133
  115.3 169.8 %all-gather.5.cloned.1.call-done = bf16[2304,3,1024]{2,0,1:T(8,128)(2,1)} async-done(((bf16[144,3,1024]{2,0,1:T(8,128)(2,1)}), bf16[2304,3,1024]{2,0,1:T(8,128)(2,1)}) %all-gather.5.cloned.1.call-update) | async-done | bytes 14155792 | tf_op jit(solution)/shard_map/all_gather | solution.py:105
  285.0 6.3 fusion.7
  291.4 5.1 fusion.48
  301.3 16.9 %all-reduce.8.cloned.1.call-done = f32[128,1024]{1,0:T(8,128)} async-done(((f32[128,1024]{1,0:T(8,128)}), f32[128,1024]{1,0:T(8,128)}) %all-reduce.8.cloned.1.call-update) | async-done | bytes 524304 | tf_op jit(solution)/shard_map/psum | solution.py:166
  324.6 7.8 reduce.12
  335.2 6.8 all-to-all-start.1
  343.6 14.7 %collective-permute-done.2 = bf16[1,2,1024]{2,1,0:T(2,128)(2,1)S(1)} collective-permute-done((bf16[1,2,1024]{2,1,0:T(2,128)(2,1)S(1)}, bf16[1,2,1024]{2,1,0:T(2,128)(2,1)S(1)}, u32[]{:S(2)}, u32[]{:S(2)}) %collective-permute-start.2) | collective-permute-done | bytes 4128 | tf_op jit(solution)/shard_map/ppermute | solution.py:19
  361.3 12.7 %collective-permute-done.1 = bf16[1,2,1024]{2,1,0:T(2,128)(2,1)S(1)} collective-permute-done((bf16[1,2,1024]{2,1,0:T(2,128)(2,1)S(1)}, bf16[1,2,1024]{2,1,0:T(2,128)(2,1)S(1)}, u32[]{:S(2)}, u32[]{:S(2)}) %collective-permute-start.1) | collective-permute-done | bytes 4128 | tf_op jit(solution)/shard_map/ppermute | solution.py:19
  379.3 7.8 copy.43
  387.1 5.2 all-to-all-start
  395.7 32.2 %copy.77 = bf16[1,2304,1024]{2,0,1:T(2,128)(2,1)} copy(bf16[1,2304,1024]{2,1,0:T(8,128)(2,1)S(1)} %fusion.4) | data formatting | bytes 9437184 | tf_op jit(solution)/shard_map/convert_element_type | solution.py:71
  427.9 29.0 %reduce.13 = bf16[2304,1024]{1,0:T(8,128)(2,1)} reduce(bf16[2304,1,1024]{2,1,0:T(2,128)(2,1)} %bitcast.200, bf16[]{:T(256)} %broadcast.107), dimensions={1}, to_apply=%bitcast.198.reduce_sub_computation | reduce | bytes 9437186
  456.9 11.8 %reshape.255 = bf16[16,2,73728]{2,1,0:T(2,128)(2,1)} reshape(bf16[2304,1024]{1,0:T(8,128)(2,1)} %reduce.13) | data formatting | bytes 9437184
  468.7 16.8 %all-to-all-done = bf16[1,512,3,1024]{3,2,0,1:T(4,128)(2,1)} async-done(((bf16[1,512,3,1024]{3,2,0,1:T(4,128)(2,1)}), bf16[1,512,3,1024]{3,2,0,1:T(4,128)(2,1)}, u32[]{:S(2)}, u32[]{:S(2)}) %all-to-all-start) | async-done | bytes 3145760 | tf_op jit(solution)/shard_map/all_to_all | solution.py:63
  485.4 4.6 all-to-all-start.3
  490.1 6.3 convert_bitcast_fusion
  496.4 23.9 %copy.47 = bf16[1,2304,2,1024]{3,2,0,1:T(2,128)(2,1)} copy(bf16[1,2304,2,1024]{1,3,2,0:T(8,128)(2,1)} %convert_bitcast_fusion) | data formatting | bytes 18874368 | tf_op jit(solution)/shard_map/convert_element_type | solution.py:64
  520.3 86.0 %all-to-all-done.3 = bf16[16,2,73728]{2,1,0:T(2,128)(2,1)} async-done(((bf16[16,2,73728]{2,1,0:T(2,128)(2,1)}), bf16[16,2,73728]{2,1,0:T(2,128)(2,1)}, u32[]{:S(2)}, u32[]{:S(2)}) %all-to-all-start.3) | async-done | bytes 4718624 | tf_op jit(solution)/shard_map/all_to_all | solution.py:70
  606.2 4.8 all-to-all-start.2
  611.3 4.0 fusion.25
  617.4 19.5 %all-reduce.10.cloned.1.call-done = (bf16[128,1024]{1,0:T(8,128)(2,1)}, bf16[128,1024]{1,0:T(8,128)(2,1)}) async-done(((bf16[128,1024]{1,0:T(8,128)(2,1)}, bf16[128,1024]{1,0:T(8,128)(2,1)}), (bf16[128,1024]{1,0:T(8,128)(2,1)}, bf16[128,1024]{1,0:T(8,128)(2,1)})) %all-reduce.10.cloned.1.call-update) | async-done | bytes 524304 | tf_op jit(solution)/shard_map/psum | solution.py:147
  638.3 216.6 %all-reduce = (f32[3,1024]{1,0:T(4,128)S(1)}, f32[2,1024]{1,0:T(2,128)S(1)}) all-reduce(f32[3,1024]{1,0:T(4,128)S(1)} %reshape.224, f32[2,1024]{1,0:T(2,128)S(1)} %pad_maximum_fusion.9), channel_id=1, replica_groups=mesh['shard'=4,'ctx'=4,'tp'=2] {'shard','ctx','tp'}, use_global_device_ids=true, to_apply=%region_15.16 | all-reduce | flops 5120 | bytes 40960 | tf_op jit(solution)/shard_map/psum | solution.py:218
  863.6 3.4 copy.44
  874.2 13.1 %reshape.256 = bf16[2304,1,1024]{2,1,0:T(2,128)(2,1)} reshape(bf16[16,2,73728]{2,1,0:T(2,128)(2,1)} %all-to-all-done.3) | data formatting | bytes 9437184
  887.2 9.6 %copy.63 = f32[1,2304,1024]{2,1,0:T(8,128)} copy(bf16[1,2304,1024]{2,0,1:T(2,128)(2,1)} %bitcast.202) | data formatting | bytes 14155776
  896.8 4.7 reduce_sum.124
  901.5 10.4 %copy.48 = bf16[1,2304,2,1024]{3,1,2,0:T(8,128)(2,1)} copy(bf16[1,2304,2,1024]{3,2,0,1:T(2,128)(2,1)} %all-to-all-done.2) | data formatting | bytes 18874368 | tf_op jit(solution)/shard_map/all_to_all | solution.py:63
  911.9 6.3 convert_reduce_fusion
  918.3 3.5 multiply_subtract_fusion
  (168 shorter events, 62.9 us)
Async XLA Ops:
  7.2 82.4 %all-gather.3.cloned.1.call-start = ((), (), s32[]{:S(2)}) async-start(), calls=%async_computation.4 | async-start | bytes 4456448 | tf_op jit(solution)/shard_map/all_gather | solution.py:104
  9.3 104.8 %all-reduce.6.cloned.1.call-start = ((), (), s32[]{:S(2)}) async-start(), calls=%async_computation.5 | async-start | bytes 1048576 | tf_op jit(solution)/shard_map/psum | solution.py:133
  11.3 309.1 %copy-start.23 = (f32[1,1024]{1,0:T(1,128)}, f32[1,1024]{1,0:T(1,128)S(1)}, u32[]{:S(2)}) copy-start(f32[1,1024]{1,0:T(1,128)S(1)} %get-tuple-element.80) | copy-start | bytes 12292
  12.9 6.3 collective-permute-start
  18.2 74.5 %copy-start.28 = (f32[512]{0:T(512)}, f32[512]{0:T(512)S(1)}, u32[]{:S(2)}) copy-start(f32[512]{0:T(512)S(1)} %mul.367) | copy-start | bytes 6148
  18.3 74.4 %copy-start.30 = (f32[512]{0:T(512)}, f32[512]{0:T(512)S(1)}, u32[]{:S(2)}) copy-start(f32[512]{0:T(512)S(1)} %mul.371) | copy-start | bytes 6148
  18.4 74.4 %copy-start.32 = (f32[512]{0:T(512)}, f32[512]{0:T(512)S(1)}, u32[]{:S(2)}) copy-start(f32[512]{0:T(512)S(1)} %mul.374) | copy-start | bytes 6148
  96.7 17.4 %copy-start = (bf16[1,128,1024]{2,1,0:T(8,128)(2,1)S(1)}, bf16[1,128,1024]{2,1,0:T(8,128)(2,1)}, u32[]{:S(2)}) copy-start(bf16[1,128,1024]{2,1,0:T(8,128)(2,1)} %param.14) | copy-start | bytes 786436
  96.7 188.3 %all-gather.5.cloned.1.call-start = ((), (), s32[]{:S(2)}) async-start(), calls=%async_computation.6 | async-start | bytes 15040512 | tf_op jit(solution)/shard_map/all_gather | solution.py:105
  97.9 220.4 %all-reduce.8.cloned.1.call-start = ((), (), s32[]{:S(2)}) async-start(), calls=%async_computation.7 | async-start | bytes 1048576 | tf_op jit(solution)/shard_map/psum | solution.py:166
  115.3 205.1 %copy-start.43 = (f32[128]{0:T(128)}, f32[128]{0:T(128)S(1)}, u32[]{:S(2)}) copy-start(f32[128]{0:T(128)S(1)} %add_rsqrt_fusion) | copy-start | bytes 1540
  335.2 51.9 %all-to-all-start.1 = ((bf16[16,2,16384]{2,1,0:T(2,128)(2,1)}), bf16[16,2,16384]{2,1,0:T(2,128)(2,1)S(1)}, u32[]{:S(2)}, u32[]{:S(2)}) async-start(bf16[16,2,16384]{2,1,0:T(2,128)(2,1)} %reshape.253), calls=%async_computation.1 | async-start | bytes 2097152 | tf_op jit(solution)/shard_map/all_to_all | solution.py:70
  342.1 17.8 %copy-start.20 = (bf16[1,128,1024]{2,1,0:T(8,128)(2,1)S(1)}, bf16[1,128,1024]{2,1,0:T(8,128)(2,1)}, u32[]{:S(2)}) copy-start(bf16[1,128,1024]{2,1,0:T(8,128)(2,1)} %get-tuple-element.65) | copy-start | bytes 786436
  342.1 16.2 %collective-permute-start.2 = (bf16[1,2,1024]{2,1,0:T(2,128)(2,1)S(1)}, bf16[1,2,1024]{2,1,0:T(2,128)(2,1)S(1)}, u32[]{:S(2)}, u32[]{:S(2)}) collective-permute-start(bf16[1,2,1024]{2,1,0:T(2,128)(2,1)S(1)} %get-tuple-element.78), channel_id=1, source_target_pairs={{2,0},{4,2},{6,4},{3,1},{5,3},{7,5},{10,8},{12,10},{14,12},{11,9},... | collective-permute-start | bytes 12296 | tf_op jit(solution)/shard_map/ppermute | solution.py:19
  359.8 16.0 %copy-start.31 = (f32[512]{0:T(512)S(1)}, f32[512]{0:T(512)}, u32[]{:S(2)}) copy-start(f32[512]{0:T(512)} %copy-done.30) | copy-start | bytes 6148
  359.8 16.0 %copy-start.33 = (f32[512]{0:T(512)S(1)}, f32[512]{0:T(512)}, u32[]{:S(2)}) copy-start(f32[512]{0:T(512)} %copy-done.32) | copy-start | bytes 6148
  359.9 14.2 %collective-permute-start.1 = (bf16[1,2,1024]{2,1,0:T(2,128)(2,1)S(1)}, bf16[1,2,1024]{2,1,0:T(2,128)(2,1)S(1)}, u32[]{:S(2)}, u32[]{:S(2)}) collective-permute-start(bf16[1,2,1024]{2,1,0:T(2,128)(2,1)S(1)} %slice.137), channel_id=1, source_target_pairs={{2,0},{4,2},{6,4},{3,1},{5,3},{7,5},{10,8},{12,10},{14,12},{11,9},... | collective-permute-start | bytes 12296 | tf_op jit(solution)/shard_map/ppermute | solution.py:19
  387.1 98.4 %all-to-all-start = ((bf16[1,512,3,1024]{3,2,0,1:T(4,128)(2,1)}), bf16[1,512,3,1024]{3,2,0,1:T(4,128)(2,1)}, u32[]{:S(2)}, u32[]{:S(2)}) async-start(bf16[1,512,3,1024]{3,2,0,1:T(4,128)(2,1)} %copy.43), calls=%async_computation | async-start | bytes 8388608 | tf_op jit(solution)/shard_map/all_to_all | solution.py:63
  468.6 21.4 %copy-start.24 = (f32[1,1024]{1,0:T(1,128)S(1)}, f32[1,1024]{1,0:T(1,128)}, u32[]{:S(2)}) copy-start(f32[1,1024]{1,0:T(1,128)} %copy-done.23) | copy-start | bytes 12292
  468.6 21.4 %copy-start.44 = (f32[128]{0:T(128)S(1)}, f32[128]{0:T(128)}, u32[]{:S(2)}) copy-start(f32[128]{0:T(128)} %copy-done.43) | copy-start | bytes 1540
  485.4 120.8 %all-to-all-start.3 = ((bf16[16,2,73728]{2,1,0:T(2,128)(2,1)}), bf16[16,2,73728]{2,1,0:T(2,128)(2,1)}, u32[]{:S(2)}, u32[]{:S(2)}) async-start(bf16[16,2,73728]{2,1,0:T(2,128)(2,1)} %reshape.255), calls=%async_computation.3 | async-start | bytes 9437184 | tf_op jit(solution)/shard_map/all_to_all | solution.py:70
  606.2 295.3 %all-to-all-start.2 = ((bf16[1,2304,2,1024]{3,2,0,1:T(2,128)(2,1)}), bf16[1,2304,2,1024]{3,2,0,1:T(2,128)(2,1)}, u32[]{:S(2)}, u32[]{:S(2)}) async-start(bf16[1,2304,2,1024]{3,2,0,1:T(2,128)(2,1)} %copy.47), calls=%async_computation.2 | async-start | bytes 18874368 | tf_op jit(solution)/shard_map/all_to_all | solution.py:63
  611.0 25.8 %all-reduce.10.cloned.1.call-start = ((), (), s32[]{:S(2)}) async-start(), calls=%async_computation.8 | async-start | bytes 1048576 | tf_op jit(solution)/shard_map/psum | solution.py:147
  616.8 21.5 %copy-start.34 = (f32[1024]{0:T(1024)S(1)}, f32[1024]{0:T(1024)}, u32[]{:S(2)}) copy-start(f32[1024]{0:T(1024)} %get-tuple-element.39) | copy-start | bytes 12292
  616.8 238.2 %copy-start.27 = (f32[2,1024]{1,0:T(2,128)S(1)}, f32[2,1024]{1,0:T(2,128)}, u32[]{:S(2)}) copy-start(f32[2,1024]{1,0:T(2,128)} %param.19) | copy-start | bytes 24580
  616.8 238.2 %copy-start.40 = (f32[2,1024]{1,0:T(2,128)S(1)}, f32[2,1024]{1,0:T(2,128)}, u32[]{:S(2)}) copy-start(f32[2,1024]{1,0:T(2,128)} %param.26) | copy-start | bytes 24580
  616.8 238.2 %copy-start.41 = (f32[2,1024]{1,0:T(2,128)S(1)}, f32[2,1024]{1,0:T(2,128)}, u32[]{:S(2)}) copy-start(f32[2,1024]{1,0:T(2,128)} %param.27) | copy-start | bytes 24580
  616.8 238.9 %copy-start.26 = (f32[3,1024]{1,0:T(4,128)S(1)}, f32[3,1024]{1,0:T(4,128)}, u32[]{:S(2)}) copy-start(f32[3,1024]{1,0:T(4,128)} %param.18) | copy-start | bytes 36868
  616.8 238.9 %copy-start.35 = (f32[3,1024]{1,0:T(4,128)S(1)}, f32[3,1024]{1,0:T(4,128)}, u32[]{:S(2)}) copy-start(f32[3,1024]{1,0:T(4,128)} %param.24) | copy-start | bytes 36868
  616.8 238.9 %copy-start.36 = (f32[3,1024]{1,0:T(4,128)S(1)}, f32[3,1024]{1,0:T(4,128)}, u32[]{:S(2)}) copy-start(f32[3,1024]{1,0:T(4,128)} %param.25) | copy-start | bytes 36868
  616.8 241.2 %copy-start.4 = (f32[128,1024]{1,0:T(8,128)S(1)}, f32[128,1024]{1,0:T(8,128)}, u32[]{:S(2)}) copy-start(f32[128,1024]{1,0:T(8,128)} %copy-done.3) | copy-start | bytes 1572868
  636.9 221.2 %copy-start.12 = (bf16[128,1024]{1,0:T(8,128)(2,1)S(1)}, bf16[128,1024]{1,0:T(8,128)(2,1)}, u32[]{:S(2)}) copy-start(bf16[128,1024]{1,0:T(8,128)(2,1)} %get-tuple-element.49) | copy-start | bytes 786436
  (26 other events, 136.0 us)
Sparse Core Ops, SparseCore 0:
  11.4 78.1 all-gather.2
  96.8 17.1 all-reduce.5
  117.5 167.4 all-gather.4
  301.4 16.7 all-reduce.7
  617.0 19.8 all-reduce.9
where the time goes:
time: 934 us; the launch traced here: 929 us
  waiting for transfers between devices  424 us (45%)
  blocking collectives  217 us (23%)
  local copies, waits for them, and re-layouts  134 us (14%)
  other arithmetic  70.8 us (8%)
  matrix products  38.6 us (4%)
  starting transfers between devices  29.7 us (3%)
  between operations  14.8 us (2%)
    psum x1, blocking collectives, per_device(): lax.psum((gain_terms, spread_taps(tap_grads, model_width)), ('shard', 'ct...  217 us
    all_gather x1, waiting for transfers between devices, per_device(): lax.all_gather(ffn_half, ('shard', 'ctx'), axis=0, tiled=True)  170 us
    all_to_all x2, waiting for transfers between devices, reduce_terms(): lax.all_to_all(outer_term[None].astype(jnp.bfloat16), ('shard', 'ctx'), s...  86 us
    all_gather x1, waiting for transfers between devices, per_device(): lax.all_gather(mixer_half, ('shard', 'ctx'), axis=0, tiled=True)  70.4 us
    unnamed x104, local copies, waits for them, and re-layouts  53.3 us
    unnamed x2, other arithmetic  36.7 us
    convert_element_type x2, local copies, waits for them, and re-layouts, reduce_terms(): outer_term[None].astype(jnp.bfloat16)  33.8 us
    convert_element_type x2, local copies, waits for them, and re-layouts, reduce_terms(): inner_term[None].astype(jnp.bfloat16)  31.7 us
  transfers between devices with their start and end apart: 12, of which 10 were waited for; matrix products, arithmetic and copies ran while one was open for 19% of the time, Pallas kernels for 0%

commit v1 on v0

--- a/solution.py
+++ b/solution.py
@@ -11,6 +11,25 @@
 matrix_rate = 0.02
 small_rate = 0.25
 decay_rate = 0.1
+
+
+def watch_the_types(arr_in, d0):
+    shard_axis = ("shard", "ctx")
+    work_now = jax.lax.axis_size(shard_axis)
+    front, v_now, main = (work_now, jax.lax.axis_index(shard_axis), arr_in.shape[d0])
+    vals = [j * front if ix == d0 else j for ix, j in enumerate(arr_in.shape)]
+    built = jnp.zeros(vals, arr_in.dtype)
+    w_next = lax.dynamic_update_slice_in_dim(built, arr_in, v_now * main, axis=d0)
+    c = 1
+    while c < front:
+        arr_in = jax.lax.ppermute(
+            arr_in, shard_axis, [(ix, (ix + 1) % front) for ix in range(front)]
+        )
+        w_next = lax.dynamic_update_slice_in_dim(
+            w_next, arr_in, (v_now - c) % front * main, axis=d0
+        )
+        c += 1
+    return w_next
 
 
 def shifted(value, axis, steps):
@@ -102,7 +121,7 @@
     ffn_half = ffn_weight.astype(jnp.bfloat16)
     mixer_whole, ffn_whole = (
         lax.all_gather(mixer_half, ("shard", "ctx"), axis=0, tiled=True),
-        lax.all_gather(ffn_half, ("shard", "ctx"), axis=0, tiled=True),
+        watch_the_types(ffn_half, 0),
     )
     channel_count = mixer_whole.shape[0]
     x_rows = inputs.reshape(row_count, model_width).astype(jnp.float32)

time: 934 us -> 1200 us (1.28)
  waiting for transfers between devices: 424 us -> 644 us
  local copies, waits for them, and re-layouts: 134 us -> 170 us
  starting transfers between devices: 29.7 us -> 42.5 us
    ppermute x0 -> x15, waiting for transfers between devices: none -> 432 us  [watch_the_types(): jax.lax.ppermute(arr_in, shard_axis, [(ix, (ix + 1) % front) for ix in ra...]
    all_gather x1, waiting for transfers between devices: 170 us -> 0.02 us  [per_device(): lax.all_gather(ffn_half, ('shard', 'ctx'), axis=0, tiled=True)]
    all_to_all x2, waiting for transfers between devices: 86 us -> 40.9 us  [reduce_terms(): lax.all_to_all(outer_term[None].astype(jnp.bfloat16), ('shard', 'ctx'), s...]
    all_to_all x2, waiting for transfers between devices: 16.8 us -> 61.2 us  [reduce_terms(): lax.all_to_all(inner_term[None].astype(jnp.bfloat16), ('shard', 'ctx'), s...]
    dynamic_update_slice x0 -> x15, local copies, waits for them, and re-layouts: none -> 19.8 us  [watch_the_types(): lax.dynamic_update_slice_in_dim(w_next, arr_in, (v_now - c) % front * mai...]
    psum x1, waiting for transfers between devices: 19.5 us -> 0.02 us  [per_device(): ffn_out = lax.psum(ffn_part.astype(jnp.bfloat16), 'tp').astype(jnp.float32)]
    psum x1, waiting for transfers between devices: 16.2 us -> 0.01 us  [per_device(): mix_out = lax.psum(mix_part, 'tp')]
    ppermute x0 -> x15, starting transfers between devices: none -> 15.2 us  [watch_the_types(): jax.lax.ppermute(arr_in, shard_axis, [(ix, (ix + 1) % front) for ix in ra...]
  transfers between devices with their start and end apart: 12 -> 27, of which waited for: 10 -> 22; matrix products, arithmetic and copies ran while one was open for 19% -> 20% of each run, Pallas kernels for 0% -> 0%
where the time goes in v1:
time: 1200 us; the launch traced here: 1190 us
  waiting for transfers between devices  644 us (54%)
  blocking collectives  212 us (18%)
  local copies, waits for them, and re-layouts  170 us (14%)
  other arithmetic  70.7 us (6%)
  starting transfers between devices  42.5 us (4%)
  matrix products  36.9 us (3%)
  between operations  15.2 us (1%)
    ppermute x15, waiting for transfers between devices, watch_the_types(): jax.lax.ppermute(arr_in, shard_axis, [(ix, (ix + 1) % front) for ix in ra...  432 us
    psum x1, blocking collectives, per_device(): lax.psum((gain_terms, spread_taps(tap_grads, model_width)), ('shard', 'ct...  212 us
    all_gather x1, waiting for transfers between devices, per_device(): lax.all_gather(mixer_half, ('shard', 'ctx'), axis=0, tiled=True)  69.8 us
    all_to_all x2, waiting for transfers between devices, reduce_terms(): lax.all_to_all(inner_term[None].astype(jnp.bfloat16), ('shard', 'ctx'), s...  61.2 us
    unnamed x148, local copies, waits for them, and re-layouts  58.5 us
    all_to_all x2, waiting for transfers between devices, reduce_terms(): lax.all_to_all(outer_term[None].astype(jnp.bfloat16), ('shard', 'ctx'), s...  40.9 us
    unnamed x2, other arithmetic  36.7 us
    convert_element_type x2, local copies, waits for them, and re-layouts, reduce_terms(): outer_term[None].astype(jnp.bfloat16)  33.8 us
  transfers between devices with their start and end apart: 27, of which 22 were waited for; matrix products, arithmetic and copies ran while one was open for 20% of the time, Pallas kernels for 0%

profile of v1, /device:TPU:0, one launch (start us, length us, event | category | flops | bytes accessed | tf_op | source)
XLA Modules:
  0.0 1191.4 jit_solution(13247738175634158952)
XLA Ops:
  19.8 69.8 %all-gather.3.cloned.1.call-done = bf16[512,4,1024]{2,0,1:T(8,128)(2,1)} async-done(((bf16[32,4,1024]{2,0,1:T(8,128)(2,1)}), bf16[512,4,1024]{2,0,1:T(8,128)(2,1)}) %all-gather.3.cloned.1.call-update) | async-done | bytes 4194320 | tf_op jit(solution)/shard_map/all_gather | solution.py:123
  96.8 6.9 broadcast_in_dim.9
  106.7 22.1 %collective-permute-done.1 = bf16[144,3,1024]{2,0,1:T(8,128)(2,1)S(1)} collective-permute-done((bf16[144,3,1024]{2,0,1:T(8,128)(2,1)}, bf16[144,3,1024]{2,0,1:T(8,128)(2,1)S(1)}, u32[]{:S(2)}, u32[]{:S(2)}) %collective-permute-start.1) | collective-permute-done | bytes 884768 | tf_op jit(solution)/shard_map/ppermute | solution.py:25
  128.8 42.0 %collective-permute-done.2 = bf16[144,3,1024]{2,0,1:T(8,128)(2,1)S(1)} collective-permute-done((bf16[144,3,1024]{2,0,1:T(8,128)(2,1)S(1)}, bf16[144,3,1024]{2,0,1:T(8,128)(2,1)S(1)}, u32[]{:S(2)}, u32[]{:S(2)}) %collective-permute-start.2) | collective-permute-done | bytes 884768 | tf_op jit(solution)/shard_map/ppermute | solution.py:25
  170.8 42.9 %collective-permute-done.3 = bf16[144,3,1024]{2,0,1:T(8,128)(2,1)S(1)} collective-permute-done((bf16[144,3,1024]{2,0,1:T(8,128)(2,1)S(1)}, bf16[144,3,1024]{2,0,1:T(8,128)(2,1)S(1)}, u32[]{:S(2)}, u32[]{:S(2)}) %collective-permute-start.3) | collective-permute-done | bytes 884768 | tf_op jit(solution)/shard_map/ppermute | solution.py:25
  214.6 35.8 %collective-permute-done.4 = bf16[144,3,1024]{2,0,1:T(8,128)(2,1)S(1)} collective-permute-done((bf16[144,3,1024]{2,0,1:T(8,128)(2,1)S(1)}, bf16[144,3,1024]{2,0,1:T(8,128)(2,1)S(1)}, u32[]{:S(2)}, u32[]{:S(2)}) %collective-permute-start.4) | collective-permute-done | bytes 884768 | tf_op jit(solution)/shard_map/ppermute | solution.py:25
  251.3 42.5 %collective-permute-done.5 = bf16[144,3,1024]{2,0,1:T(8,128)(2,1)S(1)} collective-permute-done((bf16[144,3,1024]{2,0,1:T(8,128)(2,1)S(1)}, bf16[144,3,1024]{2,0,1:T(8,128)(2,1)S(1)}, u32[]{:S(2)}, u32[]{:S(2)}) %collective-permute-start.5) | collective-permute-done | bytes 884768 | tf_op jit(solution)/shard_map/ppermute | solution.py:25
  293.9 39.3 %collective-permute-done.6 = bf16[144,3,1024]{2,0,1:T(8,128)(2,1)S(1)} collective-permute-done((bf16[144,3,1024]{2,0,1:T(8,128)(2,1)S(1)}, bf16[144,3,1024]{2,0,1:T(8,128)(2,1)S(1)}, u32[]{:S(2)}, u32[]{:S(2)}) %collective-permute-start.6) | collective-permute-done | bytes 884768 | tf_op jit(solution)/shard_map/ppermute | solution.py:25
  333.1 13.4 %collective-permute-start.7 = (bf16[144,3,1024]{2,0,1:T(8,128)(2,1)S(1)}, bf16[144,3,1024]{2,0,1:T(8,128)(2,1)S(1)}, u32[]{:S(2)}, u32[]{:S(2)}) collective-permute-start(bf16[144,3,1024]{2,0,1:T(8,128)(2,1)S(1)} %collective-permute-done.6), channel_id=1, source_target_pairs={{0,2},{2,4},{4,6},{6,8},{8,10},{10,12},{12,14},{14,16},{16,18},{18... | collective-permute-start | bytes 2654216 | tf_op jit(solution)/shard_map/ppermute | solution.py:25
  346.5 39.7 %collective-permute-done.7 = bf16[144,3,1024]{2,0,1:T(8,128)(2,1)S(1)} collective-permute-done((bf16[144,3,1024]{2,0,1:T(8,128)(2,1)S(1)}, bf16[144,3,1024]{2,0,1:T(8,128)(2,1)S(1)}, u32[]{:S(2)}, u32[]{:S(2)}) %collective-permute-start.7) | collective-permute-done | bytes 884768 | tf_op jit(solution)/shard_map/ppermute | solution.py:25
  386.2 24.9 %collective-permute-done.8 = bf16[144,3,1024]{2,0,1:T(8,128)(2,1)S(1)} collective-permute-done((bf16[144,3,1024]{2,0,1:T(8,128)(2,1)S(1)}, bf16[144,3,1024]{2,0,1:T(8,128)(2,1)S(1)}, u32[]{:S(2)}, u32[]{:S(2)}) %collective-permute-start.8) | collective-permute-done | bytes 884768 | tf_op jit(solution)/shard_map/ppermute | solution.py:25
  411.1 26.1 %collective-permute-done.9 = bf16[144,3,1024]{2,0,1:T(8,128)(2,1)S(1)} collective-permute-done((bf16[144,3,1024]{2,0,1:T(8,128)(2,1)S(1)}, bf16[144,3,1024]{2,0,1:T(8,128)(2,1)S(1)}, u32[]{:S(2)}, u32[]{:S(2)}) %collective-permute-start.9) | collective-permute-done | bytes 884768 | tf_op jit(solution)/shard_map/ppermute | solution.py:25
  437.2 25.3 %collective-permute-done.10 = bf16[144,3,1024]{2,0,1:T(8,128)(2,1)S(1)} collective-permute-done((bf16[144,3,1024]{2,0,1:T(8,128)(2,1)S(1)}, bf16[144,3,1024]{2,0,1:T(8,128)(2,1)S(1)}, u32[]{:S(2)}, u32[]{:S(2)}) %collective-permute-start.10) | collective-permute-done | bytes 884768 | tf_op jit(solution)/shard_map/ppermute | solution.py:25
  462.5 25.3 %collective-permute-done.11 = bf16[144,3,1024]{2,0,1:T(8,128)(2,1)S(1)} collective-permute-done((bf16[144,3,1024]{2,0,1:T(8,128)(2,1)S(1)}, bf16[144,3,1024]{2,0,1:T(8,128)(2,1)S(1)}, u32[]{:S(2)}, u32[]{:S(2)}) %collective-permute-start.11) | collective-permute-done | bytes 884768 | tf_op jit(solution)/shard_map/ppermute | solution.py:25
  488.8 23.9 %collective-permute-done.12 = bf16[144,3,1024]{2,0,1:T(8,128)(2,1)} collective-permute-done((bf16[144,3,1024]{2,0,1:T(8,128)(2,1)S(1)}, bf16[144,3,1024]{2,0,1:T(8,128)(2,1)}, u32[]{:S(2)}, u32[]{:S(2)}) %collective-permute-start.12) | collective-permute-done | bytes 884768 | tf_op jit(solution)/shard_map/ppermute | solution.py:25
  518.4 17.5 %collective-permute-done.13 = bf16[144,3,1024]{2,0,1:T(8,128)(2,1)} collective-permute-done((bf16[144,3,1024]{2,0,1:T(8,128)(2,1)}, bf16[144,3,1024]{2,0,1:T(8,128)(2,1)}, u32[]{:S(2)}, u32[]{:S(2)}) %collective-permute-start.13) | collective-permute-done | bytes 884768 | tf_op jit(solution)/shard_map/ppermute | solution.py:25
  542.1 16.3 %collective-permute-done.14 = bf16[144,3,1024]{2,0,1:T(8,128)(2,1)} collective-permute-done((bf16[144,3,1024]{2,0,1:T(8,128)(2,1)}, bf16[144,3,1024]{2,0,1:T(8,128)(2,1)}, u32[]{:S(2)}, u32[]{:S(2)}) %collective-permute-start.14) | collective-permute-done | bytes 884768 | tf_op jit(solution)/shard_map/ppermute | solution.py:25
  567.2 8.3 collective-permute-done.15
  584.4 32.2 %copy.92 = bf16[1,2304,1024]{2,0,1:T(2,128)(2,1)} copy(bf16[1,2304,1024]{2,1,0:T(8,128)(2,1)S(1)} %fusion.2) | data formatting | bytes 9437184 | tf_op jit(solution)/shard_map/convert_element_type | solution.py:90
  617.1 28.9 %reduce.13 = bf16[2304,1024]{1,0:T(8,128)(2,1)} reduce(bf16[2304,1,1024]{2,1,0:T(2,128)(2,1)} %bitcast.203, bf16[]{:T(256)} %broadcast.122), dimensions={1}, to_apply=%bitcast.201.reduce_sub_computation | reduce | bytes 9437186
  646.0 11.8 reshape.255
  672.7 20.0 %all-reduce.8.cloned.1.call-done = f32[128,1024]{1,0:T(8,128)} async-done(((f32[128,1024]{1,0:T(8,128)}), f32[128,1024]{1,0:T(8,128)}) %all-reduce.8.cloned.1.call-update) | async-done | bytes 524304 | tf_op jit(solution)/shard_map/psum | solution.py:185
  698.9 7.8 reduce.12
  709.7 40.9 %all-to-all-done.3 = bf16[16,2,73728]{2,1,0:T(2,128)(2,1)} async-done(((bf16[16,2,73728]{2,1,0:T(2,128)(2,1)}), bf16[16,2,73728]{2,1,0:T(2,128)(2,1)}, u32[]{:S(2)}, u32[]{:S(2)}) %all-to-all-start.3) | async-done | bytes 4718624 | tf_op jit(solution)/shard_map/all_to_all | solution.py:89
  767.0 13.8 %collective-permute-done.16 = bf16[1,2,1024]{2,1,0:T(2,128)(2,1)S(1)} collective-permute-done((bf16[1,2,1024]{2,1,0:T(2,128)(2,1)S(1)}, bf16[1,2,1024]{2,1,0:T(2,128)(2,1)S(1)}, u32[]{:S(2)}, u32[]{:S(2)}) %collective-permute-start.16) | collective-permute-done | bytes 4128 | tf_op jit(solution)/shard_map/ppermute | solution.py:38
  787.1 7.8 copy.54
  806.9 24.0 %copy.59 = bf16[1,2304,2,1024]{3,2,0,1:T(2,128)(2,1)} copy(bf16[1,2304,2,1024]{1,3,2,0:T(8,128)(2,1)} %convert_bitcast_fusion) | data formatting | bytes 18874368 | tf_op jit(solution)/shard_map/convert_element_type | solution.py:83
  830.8 61.2 %all-to-all-done = bf16[1,512,3,1024]{3,2,0,1:T(4,128)(2,1)} async-done(((bf16[1,512,3,1024]{3,2,0,1:T(4,128)(2,1)}), bf16[1,512,3,1024]{3,2,0,1:T(4,128)(2,1)}, u32[]{:S(2)}, u32[]{:S(2)}) %all-to-all-start) | async-done | bytes 3145760 | tf_op jit(solution)/shard_map/all_to_all | solution.py:82
  902.4 12.9 %reshape.256 = bf16[2304,1,1024]{2,1,0:T(2,128)(2,1)} reshape(bf16[16,2,73728]{2,1,0:T(2,128)(2,1)} %all-to-all-done.3) | data formatting | bytes 9437184
  915.4 9.7 copy.78
  932.0 211.7 %all-reduce = (f32[3,1024]{1,0:T(4,128)S(1)}, f32[2,1024]{1,0:T(2,128)S(1)}) all-reduce(f32[3,1024]{1,0:T(4,128)S(1)} %reshape.224, f32[2,1024]{1,0:T(2,128)S(1)} %pad_maximum_fusion.9), channel_id=1, replica_groups=mesh['shard'=4,'ctx'=4,'tp'=2] {'shard','ctx','tp'}, use_global_device_ids=true, to_apply=%region_15.16 | all-reduce | flops 5120 | bytes 40960 | tf_op jit(solution)/shard_map/psum | solution.py:237
  1164.5 10.4 copy.60
  (258 shorter events, 161.4 us)
Async XLA Ops:
  7.2 82.4 %all-gather.3.cloned.1.call-start = ((), (), s32[]{:S(2)}) async-start(), calls=%async_computation.4 | async-start | bytes 4456448 | tf_op jit(solution)/shard_map/all_gather | solution.py:123
  9.3 531.6 %all-reduce.6.cloned.1.call-start = ((), (), s32[]{:S(2)}) async-start(), calls=%async_computation.5 | async-start | bytes 1048576 | tf_op jit(solution)/shard_map/psum | solution.py:152
  13.5 6.3 collective-permute-start
  96.7 566.8 %all-gather.5.cloned.1.call-start = ((), (), s32[]{:S(2)}) async-start(), calls=%async_computation.6 | async-start | bytes 15040512 | tf_op jit(solution)/shard_map/all_gather | solution.py:170
  105.2 23.7 %collective-permute-start.1 = (bf16[144,3,1024]{2,0,1:T(8,128)(2,1)}, bf16[144,3,1024]{2,0,1:T(8,128)(2,1)S(1)}, u32[]{:S(2)}, u32[]{:S(2)}) collective-permute-start(bf16[144,3,1024]{2,0,1:T(8,128)(2,1)} %get-tuple-element.70), channel_id=1, source_target_pairs={{0,2},{2,4},{4,6},{6,8},{8,10},{10,12},{12,14},{14,16},{16,18},{18... | collective-permute-start | bytes 2654216 | tf_op jit(solution)/shard_map/ppermute | solution.py:25
  128.8 42.0 %collective-permute-start.2 = (bf16[144,3,1024]{2,0,1:T(8,128)(2,1)S(1)}, bf16[144,3,1024]{2,0,1:T(8,128)(2,1)S(1)}, u32[]{:S(2)}, u32[]{:S(2)}) collective-permute-start(bf16[144,3,1024]{2,0,1:T(8,128)(2,1)S(1)} %collective-permute-done.1), channel_id=1, source_target_pairs={{0,2},{2,4},{4,6},{6,8},{8,10},{10,12},{12,14},{14,16},{16,18},{18... | collective-permute-start | bytes 2654216 | tf_op jit(solution)/shard_map/ppermute | solution.py:25
  170.8 42.9 %collective-permute-start.3 = (bf16[144,3,1024]{2,0,1:T(8,128)(2,1)S(1)}, bf16[144,3,1024]{2,0,1:T(8,128)(2,1)S(1)}, u32[]{:S(2)}, u32[]{:S(2)}) collective-permute-start(bf16[144,3,1024]{2,0,1:T(8,128)(2,1)S(1)} %collective-permute-done.2), channel_id=1, source_target_pairs={{0,2},{2,4},{4,6},{6,8},{8,10},{10,12},{12,14},{14,16},{16,18},{18... | collective-permute-start | bytes 2654216 | tf_op jit(solution)/shard_map/ppermute | solution.py:25
  213.7 36.8 %collective-permute-start.4 = (bf16[144,3,1024]{2,0,1:T(8,128)(2,1)S(1)}, bf16[144,3,1024]{2,0,1:T(8,128)(2,1)S(1)}, u32[]{:S(2)}, u32[]{:S(2)}) collective-permute-start(bf16[144,3,1024]{2,0,1:T(8,128)(2,1)S(1)} %collective-permute-done.3), channel_id=1, source_target_pairs={{0,2},{2,4},{4,6},{6,8},{8,10},{10,12},{12,14},{14,16},{16,18},{18... | collective-permute-start | bytes 2654216 | tf_op jit(solution)/shard_map/ppermute | solution.py:25
  250.4 43.4 %collective-permute-start.5 = (bf16[144,3,1024]{2,0,1:T(8,128)(2,1)S(1)}, bf16[144,3,1024]{2,0,1:T(8,128)(2,1)S(1)}, u32[]{:S(2)}, u32[]{:S(2)}) collective-permute-start(bf16[144,3,1024]{2,0,1:T(8,128)(2,1)S(1)} %collective-permute-done.4), channel_id=1, source_target_pairs={{0,2},{2,4},{4,6},{6,8},{8,10},{10,12},{12,14},{14,16},{16,18},{18... | collective-permute-start | bytes 2654216 | tf_op jit(solution)/shard_map/ppermute | solution.py:25
  293.9 39.3 %collective-permute-start.6 = (bf16[144,3,1024]{2,0,1:T(8,128)(2,1)S(1)}, bf16[144,3,1024]{2,0,1:T(8,128)(2,1)S(1)}, u32[]{:S(2)}, u32[]{:S(2)}) collective-permute-start(bf16[144,3,1024]{2,0,1:T(8,128)(2,1)S(1)} %collective-permute-done.5), channel_id=1, source_target_pairs={{0,2},{2,4},{4,6},{6,8},{8,10},{10,12},{12,14},{14,16},{16,18},{18... | collective-permute-start | bytes 2654216 | tf_op jit(solution)/shard_map/ppermute | solution.py:25
  333.1 53.1 %collective-permute-start.7 = (bf16[144,3,1024]{2,0,1:T(8,128)(2,1)S(1)}, bf16[144,3,1024]{2,0,1:T(8,128)(2,1)S(1)}, u32[]{:S(2)}, u32[]{:S(2)}) collective-permute-start(bf16[144,3,1024]{2,0,1:T(8,128)(2,1)S(1)} %collective-permute-done.6), channel_id=1, source_target_pairs={{0,2},{2,4},{4,6},{6,8},{8,10},{10,12},{12,14},{14,16},{16,18},{18... | collective-permute-start | bytes 2654216 | tf_op jit(solution)/shard_map/ppermute | solution.py:25
  386.2 24.9 %collective-permute-start.8 = (bf16[144,3,1024]{2,0,1:T(8,128)(2,1)S(1)}, bf16[144,3,1024]{2,0,1:T(8,128)(2,1)S(1)}, u32[]{:S(2)}, u32[]{:S(2)}) collective-permute-start(bf16[144,3,1024]{2,0,1:T(8,128)(2,1)S(1)} %collective-permute-done.7), channel_id=1, source_target_pairs={{0,2},{2,4},{4,6},{6,8},{8,10},{10,12},{12,14},{14,16},{16,18},{18... | collective-permute-start | bytes 2654216 | tf_op jit(solution)/shard_map/ppermute | solution.py:25
  411.1 26.1 %collective-permute-start.9 = (bf16[144,3,1024]{2,0,1:T(8,128)(2,1)S(1)}, bf16[144,3,1024]{2,0,1:T(8,128)(2,1)S(1)}, u32[]{:S(2)}, u32[]{:S(2)}) collective-permute-start(bf16[144,3,1024]{2,0,1:T(8,128)(2,1)S(1)} %collective-permute-done.8), channel_id=1, source_target_pairs={{0,2},{2,4},{4,6},{6,8},{8,10},{10,12},{12,14},{14,16},{16,18},{18... | collective-permute-start | bytes 2654216 | tf_op jit(solution)/shard_map/ppermute | solution.py:25
  437.2 25.3 %collective-permute-start.10 = (bf16[144,3,1024]{2,0,1:T(8,128)(2,1)S(1)}, bf16[144,3,1024]{2,0,1:T(8,128)(2,1)S(1)}, u32[]{:S(2)}, u32[]{:S(2)}) collective-permute-start(bf16[144,3,1024]{2,0,1:T(8,128)(2,1)S(1)} %collective-permute-done.9), channel_id=1, source_target_pairs={{0,2},{2,4},{4,6},{6,8},{8,10},{10,12},{12,14},{14,16},{16,18},{18... | collective-permute-start | bytes 2654216 | tf_op jit(solution)/shard_map/ppermute | solution.py:25
  462.5 25.3 %collective-permute-start.11 = (bf16[144,3,1024]{2,0,1:T(8,128)(2,1)S(1)}, bf16[144,3,1024]{2,0,1:T(8,128)(2,1)S(1)}, u32[]{:S(2)}, u32[]{:S(2)}) collective-permute-start(bf16[144,3,1024]{2,0,1:T(8,128)(2,1)S(1)} %collective-permute-done.10), channel_id=1, source_target_pairs={{0,2},{2,4},{4,6},{6,8},{8,10},{10,12},{12,14},{14,16},{16,18},{18... | collective-permute-start | bytes 2654216 | tf_op jit(solution)/shard_map/ppermute | solution.py:25
  488.8 23.9 %collective-permute-start.12 = (bf16[144,3,1024]{2,0,1:T(8,128)(2,1)S(1)}, bf16[144,3,1024]{2,0,1:T(8,128)(2,1)}, u32[]{:S(2)}, u32[]{:S(2)}) collective-permute-start(bf16[144,3,1024]{2,0,1:T(8,128)(2,1)S(1)} %collective-permute-done.11), channel_id=1, source_target_pairs={{0,2},{2,4},{4,6},{6,8},{8,10},{10,12},{12,14},{14,16},{16,18},{18... | collective-permute-start | bytes 2654216 | tf_op jit(solution)/shard_map/ppermute | solution.py:25
  512.7 23.3 %collective-permute-start.13 = (bf16[144,3,1024]{2,0,1:T(8,128)(2,1)}, bf16[144,3,1024]{2,0,1:T(8,128)(2,1)}, u32[]{:S(2)}, u32[]{:S(2)}) collective-permute-start(bf16[144,3,1024]{2,0,1:T(8,128)(2,1)} %collective-permute-done.12), channel_id=1, source_target_pairs={{0,2},{2,4},{4,6},{6,8},{8,10},{10,12},{12,14},{14,16},{16,18},{18... | collective-permute-start | bytes 2654216 | tf_op jit(solution)/shard_map/ppermute | solution.py:25
  536.0 22.5 %collective-permute-start.14 = (bf16[144,3,1024]{2,0,1:T(8,128)(2,1)}, bf16[144,3,1024]{2,0,1:T(8,128)(2,1)}, u32[]{:S(2)}, u32[]{:S(2)}) collective-permute-start(bf16[144,3,1024]{2,0,1:T(8,128)(2,1)} %collective-permute-done.13), channel_id=1, source_target_pairs={{0,2},{2,4},{4,6},{6,8},{8,10},{10,12},{12,14},{14,16},{16,18},{18... | collective-permute-start | bytes 2654216 | tf_op jit(solution)/shard_map/ppermute | solution.py:25
  558.5 17.0 %collective-permute-start.15 = (bf16[144,3,1024]{2,0,1:T(8,128)(2,1)}, bf16[144,3,1024]{2,0,1:T(8,128)(2,1)S(1)}, u32[]{:S(2)}, u32[]{:S(2)}) collective-permute-start(bf16[144,3,1024]{2,0,1:T(8,128)(2,1)} %collective-permute-done.14), channel_id=1, source_target_pairs={{0,2},{2,4},{4,6},{6,8},{8,10},{10,12},{12,14},{14,16},{16,18},{18... | collective-permute-start | bytes 2654216 | tf_op jit(solution)/shard_map/ppermute | solution.py:25
  657.8 92.8 %all-to-all-start.3 = ((bf16[16,2,73728]{2,1,0:T(2,128)(2,1)}), bf16[16,2,73728]{2,1,0:T(2,128)(2,1)}, u32[]{:S(2)}, u32[]{:S(2)}) async-start(bf16[16,2,73728]{2,1,0:T(2,128)(2,1)} %reshape.255), calls=%async_computation.3 | async-start | bytes 9437184 | tf_op jit(solution)/shard_map/all_to_all | solution.py:89
  663.2 29.5 %all-reduce.8.cloned.1.call-start = ((), (), s32[]{:S(2)}) async-start(), calls=%async_computation.7 | async-start | bytes 1048576 | tf_op jit(solution)/shard_map/psum | solution.py:185
  750.6 44.3 %all-to-all-start.1 = ((bf16[16,2,16384]{2,1,0:T(2,128)(2,1)}), bf16[16,2,16384]{2,1,0:T(2,128)(2,1)S(1)}, u32[]{:S(2)}, u32[]{:S(2)}) async-start(bf16[16,2,16384]{2,1,0:T(2,128)(2,1)} %reshape.253), calls=%async_computation.1 | async-start | bytes 2097152 | tf_op jit(solution)/shard_map/all_to_all | solution.py:89
  754.3 8.7 collective-permute-start.17
  764.7 16.1 %collective-permute-start.16 = (bf16[1,2,1024]{2,1,0:T(2,128)(2,1)S(1)}, bf16[1,2,1024]{2,1,0:T(2,128)(2,1)S(1)}, u32[]{:S(2)}, u32[]{:S(2)}) collective-permute-start(bf16[1,2,1024]{2,1,0:T(2,128)(2,1)S(1)} %slice.144), channel_id=1, source_target_pairs={{2,0},{4,2},{6,4},{3,1},{5,3},{7,5},{10,8},{12,10},{14,12},{11,9},... | collective-permute-start | bytes 12296 | tf_op jit(solution)/shard_map/ppermute | solution.py:38
  794.9 97.1 %all-to-all-start = ((bf16[1,512,3,1024]{3,2,0,1:T(4,128)(2,1)}), bf16[1,512,3,1024]{3,2,0,1:T(4,128)(2,1)}, u32[]{:S(2)}, u32[]{:S(2)}) async-start(bf16[1,512,3,1024]{3,2,0,1:T(4,128)(2,1)} %copy.54), calls=%async_computation | async-start | bytes 8388608 | tf_op jit(solution)/shard_map/all_to_all | solution.py:82
  892.0 272.5 %all-to-all-start.2 = ((bf16[1,2304,2,1024]{3,2,0,1:T(2,128)(2,1)}), bf16[1,2304,2,1024]{3,2,0,1:T(2,128)(2,1)}, u32[]{:S(2)}, u32[]{:S(2)}) async-start(bf16[1,2304,2,1024]{3,2,0,1:T(2,128)(2,1)} %copy.59), calls=%async_computation.2 | async-start | bytes 18874368 | tf_op jit(solution)/shard_map/all_to_all | solution.py:82
  896.8 33.7 %all-reduce.10.cloned.1.call-start = ((), (), s32[]{:S(2)}) async-start(), calls=%async_computation.8 | async-start | bytes 1048576 | tf_op jit(solution)/shard_map/psum | solution.py:166
  925.1 218.6 %copy-start.43 = (f32[2,1024]{1,0:T(2,128)S(1)}, f32[2,1024]{1,0:T(2,128)}, u32[]{:S(2)}) copy-start(f32[2,1024]{1,0:T(2,128)} %param.19) | copy-start | bytes 24580
  925.1 219.2 %copy-start.42 = (f32[3,1024]{1,0:T(4,128)S(1)}, f32[3,1024]{1,0:T(4,128)}, u32[]{:S(2)}) copy-start(f32[3,1024]{1,0:T(4,128)} %param.18) | copy-start | bytes 36868
  925.2 219.2 %copy-start.51 = (f32[3,1024]{1,0:T(4,128)S(1)}, f32[3,1024]{1,0:T(4,128)}, u32[]{:S(2)}) copy-start(f32[3,1024]{1,0:T(4,128)} %param.24) | copy-start | bytes 36868
  925.2 219.2 %copy-start.52 = (f32[3,1024]{1,0:T(4,128)S(1)}, f32[3,1024]{1,0:T(4,128)}, u32[]{:S(2)}) copy-start(f32[3,1024]{1,0:T(4,128)} %param.25) | copy-start | bytes 36868
  925.2 221.6 %copy-start.4 = (f32[128,1024]{1,0:T(8,128)S(1)}, f32[128,1024]{1,0:T(8,128)}, u32[]{:S(2)}) copy-start(f32[128,1024]{1,0:T(8,128)} %copy-done.3) | copy-start | bytes 1572868
  (63 other events, 2080.7 us)
Sparse Core Ops, SparseCore 0:
  11.4 78.1 all-gather.2
  96.8 17.1 all-reduce.5
  117.5 260.7 all-gather.4
  672.8 19.8 all-reduce.7
  902.5 19.8 all-reduce.9
